TPU v7x, 256 devices: a whole 4x4x8 slice. The times are simulated.
256 devices in a mesh: seq: 32 (over x, y, core), head: 8 (over z).
Axes of the slice: x: 4, y: 4, z: 8, core: 2. Of those that a mesh axis runs over, the one named last changes fastest.
Arguments:
- new_states: bfloat16 [96, 1024], replicated, may hold values from -6 to 6
- lengths: int32 [24], replicated, may hold values from 1 to 16380, as said below
- cache_keys: bfloat16 [24, 16384, 1024], P(None, 'seq', 'head'), may hold values from -3000 to 3000
- cache_values: bfloat16 [24, 16384, 1024], P(None, 'seq', 'head'), may hold values from -6 to 6
- buckets: int32 [24, 4, 16384], P(None, None, 'seq'), may hold values from 0 to 31, as said below
- attn_gain: float32 [1024], replicated, may hold values from 0.25 to 1.75
- w_query: bfloat16 [1024, 1024], P(None, 'head'), may hold values from -0.0234375 to 0.0234375
- w_key: bfloat16 [1024, 1024], P(None, 'head'), may hold values from -0.1875 to 0.1875
- w_value: bfloat16 [1024, 1024], P(None, 'head'), may hold values from -0.1875 to 0.1875
- rel_bias: float32 [32, 16], P(None, 'head'), may hold values from -27 to 2
- w_out: bfloat16 [1024, 1024], P('head'), may hold values from -0.1875 to 0.1875
- ffn_gain: float32 [1024], replicated, may hold values from 0.25 to 1.75
- w_router: float32 [1024, 16], replicated, may hold values from -0.1875 to 0.1875
- w_gate: bfloat16 [16, 1024, 2816], P('head', None, 'seq'), may hold values from -0.1875 to 0.1875
- w_up: bfloat16 [16, 1024, 2816], P('head', None, 'seq'), may hold values from -0.1875 to 0.1875
- w_down: bfloat16 [16, 2816, 1024], P('head', 'seq'), may hold values from -0.109375 to 0.109375
- expert_picks: int32 [4, 24, 2], replicated, may hold values from 0 to 15, all different within a row; in each aligned block of 24 rows (0 to 23, 24 to 47, ..., all dimensions but the last counted through in order) at most 4 rows name the same one
- final_gain: float32 [1024], replicated, may hold values from 0.25 to 1.75
- w_vocab: bfloat16 [1024, 32128], P(None, 'seq'), may hold values from -0.5 to 0.5
Outputs:
- final_hidden: bfloat16 [96, 1024], P('head')
- hidden_norm: float32 [96], P('head')
- logit_max: float32 [96], P('head')
Inputs may be any that keep to these rules, and one draw needn't show every extreme that they name: `lengths`: some request has exactly 16380 cached positions. buckets[r, t, p] is the T5 relative position bucket (16 exact buckets, then logarithmic up to a distance of 128) of the distance lengths[r] + t - p where that is not negative, else 0. `expert_picks`: A request's two picks at a step differ; at each step no expert is picked by more than 4 requests, a bound that some block reaches.
All inputs are finite; a program needn't handle non-finite values.
Results may differ from a plain program's by a relative error of at most 0.0096.
Values may be sent and summed in bfloat16 or wider, within the bound.
A program may use at most 64 MiB of HBM per device.

v0:
```python
import jax
import jax.numpy as jnp
from jax import lax
from jax.sharding import PartitionSpec as P

CAP = 4


def joined(part, axis, combine):
    gathered = jax.tree.map(lambda a: lax.all_gather(a, axis), part)

    def take(source):
        return jax.tree.map(lambda a: lax.dynamic_index_in_dim(a, source, 0, False), gathered)

    return lax.fori_loop(
        1, lax.axis_size(axis), lambda source, state: combine(state, take(source)), take(0)
    )


def norm_parts(values, gain_row):
    norm_root = jnp.sqrt(jnp.mean(values * values, axis=-1, keepdims=True) + 1e-06)
    return (values / norm_root * gain_row, norm_root[..., 0])


def join_three(earlier_part, later_part):
    joint_top = jnp.maximum(earlier_part[0], later_part[0])
    lead_scale = jnp.exp(earlier_part[0] - joint_top)
    trail_scale = jnp.exp(later_part[0] - joint_top)
    mass = earlier_part[1] * lead_scale + later_part[1] * trail_scale
    weighted = earlier_part[2] * lead_scale[..., None] + later_part[2] * trail_scale[..., None]
    return (joint_top, mass, weighted)


def shards(
    new_states,
    lengths,
    cache_keys,
    cache_values,
    buckets,
    attn_gain,
    w_query,
    w_key,
    w_value,
    rel_bias,
    w_out,
    ffn_gain,
    w_router,
    w_gate,
    w_up,
    w_down,
    expert_picks,
    final_gain,
    w_vocab,
):
    seq_count = lax.axis_size("seq")
    head_count = lax.axis_size("head")
    seq_index = lax.axis_index("seq")
    head_index = lax.axis_index("head")
    requests, span_local, inner_local = cache_keys.shape
    tokens = new_states.shape[0]
    step_count = tokens // requests
    bucket_count, heads_local = rel_bias.shape
    head_dim = inner_local // heads_local
    states = new_states.astype(jnp.float32)
    scaled, _ = norm_parts(states, attn_gain)
    scaled = scaled.astype(jnp.bfloat16)
    queries = (
        jnp.dot(scaled, w_query, preferred_element_type=jnp.float32)
        .astype(jnp.bfloat16)
        .reshape(requests, step_count, heads_local, head_dim)
    )
    key_new = (
        jnp.dot(scaled, w_key, preferred_element_type=jnp.float32)
        .astype(jnp.bfloat16)
        .reshape(requests, step_count, inner_local)
    )
    value_new = (
        jnp.dot(scaled, w_value, preferred_element_type=jnp.float32)
        .astype(jnp.bfloat16)
        .reshape(requests, step_count, inner_local)
    )
    position = seq_index * span_local + jnp.arange(span_local, dtype=jnp.int32)
    target = lengths[:, None] + jnp.arange(step_count, dtype=jnp.int32)[None, :]
    landing = position[None, None, :] == target[:, :, None]
    landed = jnp.any(landing, axis=1)[:, :, None]
    landing_low = landing.astype(jnp.bfloat16)
    placed_keys = jnp.einsum(
        "rtp,rtc->rpc", landing_low, key_new, preferred_element_type=jnp.float32
    ).astype(jnp.bfloat16)
    placed_values = jnp.einsum(
        "rtp,rtc->rpc", landing_low, value_new, preferred_element_type=jnp.float32
    ).astype(jnp.bfloat16)
    key_rows = jnp.where(landed, placed_keys, cache_keys).reshape(
        requests, span_local, heads_local, head_dim
    )
    value_rows = jnp.where(landed, placed_values, cache_values).reshape(
        requests, span_local, heads_local, head_dim
    )
    scores = jnp.einsum("rthd,rphd->rthp", queries, key_rows, preferred_element_type=jnp.float32)
    bucket_hot = (buckets[..., None] == jnp.arange(bucket_count, dtype=jnp.int32)).astype(
        jnp.float32
    )
    scores = scores + jnp.einsum(
        "rtpb,bh->rthp", bucket_hot, rel_bias, precision=lax.Precision.HIGHEST
    )
    allowed = (position[None, None, :] <= target[:, :, None])[:, :, None, :]
    scores = jnp.where(allowed, scores, -1e30)
    local_top = jnp.max(scores, axis=-1)
    weights = jnp.where(allowed, jnp.exp(scores - local_top[..., None]), 0.0)
    local_mass = jnp.sum(weights, axis=-1)
    partial_value = jnp.einsum(
        "rthp,rphd->rthd", weights, value_rows.astype(jnp.float32), precision=lax.Precision.HIGHEST
    )
    out_rows = w_out.astype(jnp.float32)
    global_top, global_mass, summed = joined(
        (local_top, local_mass, partial_value), "seq", join_three
    )
    heads_out = (summed / global_mass[..., None]).reshape(tokens, inner_local)
    projected = jnp.dot(heads_out, out_rows, precision=lax.Precision.HIGHEST)
    mixed_rows = lax.psum(projected, "head")
    hidden_one = states + mixed_rows
    normed, _ = norm_parts(hidden_one, ffn_gain)
    router_logits = jnp.dot(normed, w_router, precision=lax.Precision.HIGHEST)
    normed_low = normed.astype(jnp.bfloat16)
    expert_total = w_router.shape[1]
    local_experts, model_width, units_local = w_gate.shape
    expert_ids = jnp.arange(expert_total, dtype=jnp.int32)
    pick_marks = (expert_picks[..., None] == expert_ids).astype(jnp.int32)
    per_step = jnp.sum(pick_marks, axis=2)
    earlier = jnp.cumsum(per_step, axis=1) - per_step
    slot_index = jnp.sum(pick_marks * earlier[:, :, None, :], axis=-1)
    pick_total = expert_picks.shape[2]
    token_picks = jnp.transpose(expert_picks, (1, 0, 2)).reshape(tokens, pick_total)
    token_slots = jnp.transpose(slot_index, (1, 0, 2)).reshape(tokens, pick_total)
    token_steps = jnp.arange(tokens, dtype=jnp.int32) % step_count
    picked = jnp.sum(
        jnp.where(token_picks[..., None] == expert_ids, router_logits[:, None, :], 0.0), axis=-1
    )
    gate_first = jax.nn.sigmoid(picked[:, 0] - picked[:, 1])
    gate_second = jax.nn.sigmoid(picked[:, 1] - picked[:, 0])
    slot_rows = step_count * CAP
    row_ids = jnp.arange(local_experts * slot_rows, dtype=jnp.int32)
    row_expert = head_index * local_experts + row_ids // slot_rows
    row_step = row_ids // CAP % step_count
    row_slot = row_ids % CAP
    chooser = jnp.zeros((row_ids.shape[0], tokens), jnp.float32)
    for pick_rank in range(pick_total):
        matched = (
            (row_expert[:, None] == token_picks[None, :, pick_rank])
            & (row_step[:, None] == token_steps[None, :])
            & (row_slot[:, None] == token_slots[None, :, pick_rank])
        )
        chooser = chooser + matched.astype(jnp.float32)
    routed = jnp.dot(
        chooser.astype(jnp.bfloat16), normed_low, preferred_element_type=jnp.float32
    ).astype(jnp.bfloat16)
    routed = routed.reshape(local_experts, slot_rows, model_width)
    gate_part = jnp.einsum("esd,edf->esf", routed, w_gate, preferred_element_type=jnp.float32)
    up_part = jnp.einsum("esd,edf->esf", routed, w_up, preferred_element_type=jnp.float32)
    hidden_units = (jax.nn.gelu(gate_part, approximate=True) * up_part).astype(jnp.bfloat16)
    down_part = jnp.einsum("esf,efd->esd", hidden_units, w_down, preferred_element_type=jnp.float32)
    expert_share = lax.psum_scatter(down_part, "seq", scatter_dimension=2, tiled=True).astype(
        jnp.bfloat16
    )
    share_width = expert_share.shape[2]
    collected = lax.all_gather(expert_share[None], ("seq", "head"), axis=0, tiled=True)
    arranged = collected.reshape(seq_count, head_count, local_experts, slot_rows, share_width)
    arranged = jnp.transpose(arranged, (1, 2, 3, 0, 4)).reshape(
        expert_total * slot_rows, seq_count * share_width
    )
    group_size = tokens // head_count
    first_row = head_index * group_size
    own_picks = lax.dynamic_slice_in_dim(token_picks, first_row, group_size, 0)
    own_slots = lax.dynamic_slice_in_dim(token_slots, first_row, group_size, 0)
    own_steps = lax.dynamic_slice_in_dim(token_steps, first_row, group_size, 0)
    own_first = lax.dynamic_slice_in_dim(gate_first, first_row, group_size, 0)
    own_second = lax.dynamic_slice_in_dim(gate_second, first_row, group_size, 0)
    own_hidden = lax.dynamic_slice_in_dim(hidden_one, first_row, group_size, 0)
    flat_rows = own_picks * slot_rows + own_steps[:, None] * CAP + own_slots
    every_row = jnp.arange(expert_total * slot_rows, dtype=jnp.int32)
    select_first = (flat_rows[:, 0:1] == every_row[None, :]).astype(jnp.bfloat16)
    select_second = (flat_rows[:, 1:2] == every_row[None, :]).astype(jnp.bfloat16)
    expert_mix = own_first[:, None] * jnp.dot(
        select_first, arranged, preferred_element_type=jnp.float32
    )
    expert_mix = expert_mix + own_second[:, None] * jnp.dot(
        select_second, arranged, preferred_element_type=jnp.float32
    )
    final_rows = (own_hidden + expert_mix).astype(jnp.bfloat16)
    scaled_out, norm_root = norm_parts(final_rows.astype(jnp.float32), final_gain)
    logits = jnp.dot(scaled_out.astype(jnp.bfloat16), w_vocab, preferred_element_type=jnp.float32)
    top_logit = lax.pmax(jnp.max(logits, axis=-1), "seq")
    return (final_rows, norm_root, top_logit)


def solution(mesh):
    placed = (
        P(),
        P(),
        P(None, "seq", "head"),
        P(None, "seq", "head"),
        P(None, None, "seq"),
        P(),
        P(None, "head"),
        P(None, "head"),
        P(None, "head"),
        P(None, "head"),
        P("head", None),
        P(),
        P(),
        P("head", None, "seq"),
        P("head", None, "seq"),
        P("head", "seq", None),
        P(),
        P(),
        P(None, "seq"),
    )
    return jax.shard_map(
        shards,
        mesh=mesh,
        in_specs=placed,
        out_specs=(P("head", None), P("head"), P("head")),
        check_vma=False,
    )
```

profile of v0, /device:TPU:32, one launch (start us, length us, event | category | flops | bytes accessed | tf_op | source)
XLA Modules:
  0.0 482.6 jit_solution(6117893066806250847)
XLA Ops:
  7.3 1.2 fusion.13
  8.5 0.7 iota_add_fusion
  9.2 1.3 convolution_convert_fusion.2
  10.7 1.3 convolution_convert_fusion.1
  12.3 4.6 copy.74
  17.0 4.7 copy.77
  22.0 2.0 fusion.4
  24.0 3.1 convert_select_fusion.1
  27.1 1.0 convert_select_fusion
  28.8 3.3 convolution_bitcast_fusion.1
  33.2 25.3 %all-gather.1 = f32[768,4,2]{1,2,0:T(2,128)S(1)} all-gather(f32[24,4,2]{1,2,0:T(2,128)S(1)} %fusion.16), channel_id=3, replica_groups=mesh['seq'=32,'head'=8] {'seq'}, dimensions={0}, use_global_device_ids=true | all-gather | bytes 25344 | tf_op jit(solution)/shard_map/all_gather | solution.py:10
  59.2 25.2 %all-gather = f32[768,4,2]{1,2,0:T(2,128)S(1)} all-gather(f32[24,4,2]{1,2,0:T(2,128)S(1)} %get-tuple-element.240), channel_id=2, replica_groups=mesh['seq'=32,'head'=8] {'seq'}, dimensions={0}, use_global_device_ids=true | all-gather | bytes 25344 | tf_op jit(solution)/shard_map/all_gather | solution.py:10
  84.4 1.2 copy.83
  86.0 0.9 slice.42
  87.0 76.0 %while.19 = (s32[]{:T(128)}, f32[24,4,2]{0,2,1:T(2,128)S(1)}, f32[24,4,2]{0,2,1:T(2,128)S(1)}, f32[24,4,2,64]{3,2,1,0:T(2,128)S(1)}, f32[32,24,4,2]{1,3,2,0:T(2,...) while((s32[]{:T(128)}, f32[24,4,2]{0,2,1:T(2,128)S(1)}, ...), condition=%wide.region_5.6_spmd, body=%wide.region_4.5_spmd.sunk | while | flops 38021 | bytes 256655 | solution.py:15
  87.9 0.9 constant_dynamic-slice_fusion.6
  90.4 0.9 constant_dynamic-slice_fusion.6
  92.8 0.9 constant_dynamic-slice_fusion.6
  95.3 0.9 constant_dynamic-slice_fusion.6
  97.7 0.9 constant_dynamic-slice_fusion.6
  100.2 0.9 constant_dynamic-slice_fusion.6
  101.7 0.7 fusion.99
  102.6 0.9 constant_dynamic-slice_fusion.6
  105.1 0.9 constant_dynamic-slice_fusion.6
  107.6 0.9 constant_dynamic-slice_fusion.6
  110.0 0.9 constant_dynamic-slice_fusion.6
  112.5 0.9 constant_dynamic-slice_fusion.6
  114.9 0.9 constant_dynamic-slice_fusion.6
  117.4 0.9 constant_dynamic-slice_fusion.6
  119.8 0.9 constant_dynamic-slice_fusion.6
  121.4 0.7 fusion.99
  122.3 0.9 constant_dynamic-slice_fusion.6
  124.7 0.9 constant_dynamic-slice_fusion.6
  127.2 0.9 constant_dynamic-slice_fusion.6
  129.6 0.9 constant_dynamic-slice_fusion.6
  132.1 0.9 constant_dynamic-slice_fusion.6
  134.5 0.9 constant_dynamic-slice_fusion.6
  137.0 0.9 constant_dynamic-slice_fusion.6
  138.5 0.7 fusion.99
  139.4 0.9 constant_dynamic-slice_fusion.6
  141.9 0.9 constant_dynamic-slice_fusion.6
  144.3 0.9 constant_dynamic-slice_fusion.6
  146.8 0.9 constant_dynamic-slice_fusion.6
  149.2 0.9 constant_dynamic-slice_fusion.6
  151.7 0.9 constant_dynamic-slice_fusion.6
  154.1 0.9 constant_dynamic-slice_fusion.6
  156.6 0.9 constant_dynamic-slice_fusion.6
  158.1 0.7 fusion.99
  159.0 0.9 constant_dynamic-slice_fusion.6
  161.5 0.9 constant_dynamic-slice_fusion.6
  163.4 1.1 fusion.77
  164.6 72.5 %all-reduce.2.cloned.1.call-done = f32[96,1024]{1,0:T(8,128)} async-done(((f32[96,1024]{1,0:T(8,128)}), f32[96,1024]{1,0:T(8,128)}) %all-reduce.2.cloned.1.call-update) | async-done | bytes 393232 | tf_op jit(solution)/shard_map/psum | solution.py:120
  237.1 1.1 multiply_reduce_fusion
  239.1 1.2 fusion.78
  240.3 2.0 fusion.12
  242.3 1.3 copy.98
  243.6 1.4 reshape.208
  245.2 83.7 %reduce-scatter.4.cloned.1.call-done = f32[32,32]{1,0:T(8,128)} async-done(((f32[1024,32]{1,0:T(8,128)}), f32[32,32]{1,0:T(8,128)}) %reduce-scatter.4.cloned.1.call-update) | async-done | bytes 4112
  328.9 0.8 reshape.209
  329.8 73.4 %all-gather.3 = bf16[512,16,32]{2,1,0:T(8,128)(2,1)S(1)} all-gather(bf16[2,16,32]{2,1,0:T(8,128)(2,1)S(1)} %copy.99), channel_id=5, replica_groups=mesh['seq'=32,'head'=8] {'seq','head'}, dimensions={0}, use_global_device_ids=true | all-gather | bytes 526336 | tf_op jit(solution)/shard_map/all_gather | solution.py:166
  403.2 2.7 copy.112
  405.9 3.5 reshape.189
  410.0 0.8 convolution_reduce_fusion
  410.8 65.3 %pmax.7 = f32[12]{0:T(128)} all-reduce(f32[12]{0:T(128)S(1)} %convolution_reduce_fusion), channel_id=1, replica_groups=mesh['seq'=32,'head'=8] {'seq'}, use_global_device_ids=true, to_apply=%region_15.16 | all-reduce | flops 12 | bytes 96 | tf_op jit(solution)/shard_map/pmax | solution.py:192
  (201 shorter events, 50.4 us)
Async XLA Ops:
  7.2 402.9 %copy-start = (bf16[1024,1004]{0,1:T(8,128)(2,1)S(1)}, bf16[1024,1004]{0,1:T(8,128)(2,1)}, u32[]{:S(2)}) copy-start(bf16[1024,1004]{0,1:T(8,128)(2,1)} %param.39) | copy-start | bytes 6168580
  7.2 4.8 copy-start.2
  7.2 4.8 copy-start.12
  7.2 4.8 copy-start.9
  7.2 78.8 %all-gather.6.cloned.1.call-start = ((), (), s32[]{:S(2)}) async-start(), calls=%async_computation.2 | async-start | bytes 3244032 | tf_op jit(solution)/shard_map/all_gather | solution.py:10
  16.9 5.0 %copy-start.10 = (s32[24,4,512]{2,1,0:T(4,128)S(1)}, s32[24,4,512]{2,1,0:T(4,128)}, u32[]{:S(2)}) copy-start(s32[24,4,512]{2,1,0:T(4,128)} %param.25) | copy-start | bytes 589828
  17.0 5.0 %copy-start.14 = (f32[32,2]{0,1:T(2,128)S(1)}, f32[32,2]{0,1:T(2,128)}, u32[]{:S(2)}) copy-start(f32[32,2]{0,1:T(2,128)} %param.30) | copy-start | bytes 772
  24.0 3.1 copy-start.1
  28.8 3.3 copy-start.6
  32.1 205.0 %all-reduce.2.cloned.1.call-start = ((), (), s32[]{:S(2)}) async-start(), calls=%async_computation.1 | async-start | bytes 786432 | tf_op jit(solution)/shard_map/psum | solution.py:120
  59.1 104.3 %copy-start.4 = (bf16[128,1024]{1,0:T(8,128)(2,1)S(1)}, bf16[128,1024]{1,0:T(8,128)(2,1)}, u32[]{:S(2)}) copy-start(bf16[128,1024]{1,0:T(8,128)(2,1)} %param.31) | copy-start | bytes 786436
  86.9 151.3 %copy-start.11 = (f32[1024,16]{0,1:T(8,128)S(1)}, f32[1024,16]{0,1:T(8,128)}, u32[]{:S(2)}) copy-start(f32[1024,16]{0,1:T(8,128)} %param.33) | copy-start | bytes 196612
  87.0 151.3 %copy-start.13 = (f32[1024]{0:T(1024)S(1)}, f32[1024]{0:T(1024)}, u32[]{:S(2)}) copy-start(f32[1024]{0:T(1024)} %param.32) | copy-start | bytes 12292
  163.0 77.3 %copy-start.3 = (bf16[2,88,1024]{2,1,0:T(8,128)(2,1)S(1)}, bf16[2,88,1024]{2,1,0:T(8,128)(2,1)}, u32[]{:S(2)}) copy-start(bf16[2,88,1024]{2,1,0:T(8,128)(2,1)} %param.36) | copy-start | bytes 1081348
  164.5 164.3 %reduce-scatter.4.cloned.1.call-start = ((), (), s32[]{:S(2)}) async-start(), calls=%async_computation.3 | async-start | bytes 540672
  403.2 6.8 %copy-start.7 = (f32[1024]{0:T(1024)S(1)}, f32[1024]{0:T(1024)}, u32[]{:S(2)}) copy-start(f32[1024]{0:T(1024)} %param.38) | copy-start | bytes 12292
  410.0 66.1 %copy-start.5 = (bf16[12,1024]{1,0:T(8,128)(2,1)}, bf16[12,1024]{1,0:T(8,128)(2,1)S(1)}, u32[]{:S(2)}) copy-start(bf16[12,1024]{1,0:T(8,128)(2,1)S(1)} %get-tuple-element.243) | copy-start | bytes 73732
  410.0 66.1 %copy-start.8 = (f32[12]{0:T(128)}, f32[12]{0:T(128)S(1)}, u32[]{:S(2)}) copy-start(f32[12]{0:T(128)S(1)} %add_sqrt_fusion) | copy-start | bytes 148
Sparse Core Ops, SparseCore 0:
  32.2 53.7 all-gather.5
  164.6 72.4 all-reduce.1
  245.2 83.6 reduce-scatter.3
where the time goes:
time: 485 us; the launch traced here: 483 us
  blocking collectives  189 us (39%)
  waiting for transfers between devices  156 us (32%)
  local copies, waits for them, and re-layouts  58.1 us (12%)
  other arithmetic  44.9 us (9%)
  matrix products  19.3 us (4%)
  between operations  14.1 us (3%)
    unnamed x4, waiting for transfers between devices  83.7 us
    all_gather x1, blocking collectives, shards(): lax.all_gather(expert_share[None], ('seq', 'head'), axis=0, tiled=True)  73.4 us
    psum x1, waiting for transfers between devices, shards(): mixed_rows = lax.psum(projected, 'head')  72.5 us
    pmax x1, blocking collectives, shards(): top_logit = lax.pmax(jnp.max(logits, axis=-1), 'seq')  65.3 us
    all_gather x2, blocking collectives, joined(): gathered = jax.tree.map(lambda a: lax.all_gather(a, axis), part)  50.5 us
    dynamic_slice x34, local copies, waits for them, and re-layouts, take(): lax.dynamic_index_in_dim(a, source, 0, False)  28.9 us
    add x31, other arithmetic, join_three(): mass = earlier_part[1] * lead_scale + later_part[1] * trail_scale  21.9 us
    add x31, other arithmetic, join_three(): earlier_part[2] * lead_scale[..., None]  18.8 us
  transfers between devices with their start and end apart: 3, of which 3 were waited for; matrix products, arithmetic and copies ran while one was open for 1% of the time, Pallas kernels for 0%

commit v1 on v0

--- a/solution.py
+++ b/solution.py
@@ -1,9 +1,24 @@
+import functools
 import jax
 import jax.numpy as jnp
 from jax import lax
 from jax.sharding import PartitionSpec as P
+from jax.lax import axis_size, ppermute
 
 CAP = 4
+
+
+def open_points(local_values, row_axis):
+    n_dev_all = axis_size(row_axis)
+    step_out = lambda shaped: [(q, q ^ shaped) for q in range(n_dev_all)]
+    part_now = local_values
+    for p in range(n_dev_all.bit_length() - 1):
+        all_rows = ppermute(part_now, row_axis, step_out(1 << p))
+        part_now = part_now + all_rows
+    return part_now
+
+
+choose_layers_all = functools.partial(open_points, row_axis="head")
 
 
 def joined(part, axis, combine):
@@ -117,7 +132,7 @@
     )
     heads_out = (summed / global_mass[..., None]).reshape(tokens, inner_local)
     projected = jnp.dot(heads_out, out_rows, precision=lax.Precision.HIGHEST)
-    mixed_rows = lax.psum(projected, "head")
+    mixed_rows = choose_layers_all(projected)
     hidden_one = states + mixed_rows
     normed, _ = norm_parts(hidden_one, ffn_gain)
     router_logits = jnp.dot(normed, w_router, precision=lax.Precision.HIGHEST)

time: 485 us -> 463 us (0.955)
  waiting for transfers between devices: 156 us -> 128 us
  starting transfers between devices: 0.12 us -> 8.15 us
    psum x1 -> x0, waiting for transfers between devices: 72.5 us -> none  [shards(): mixed_rows = lax.psum(projected, 'head')]
    ppermute x0 -> x3, waiting for transfers between devices: none -> 39.4 us  [open_points(): all_rows = ppermute(part_now, row_axis, step_out(1 << p))]
    ppermute x0 -> x3, starting transfers between devices: none -> 8.07 us  [open_points(): all_rows = ppermute(part_now, row_axis, step_out(1 << p))]
    unnamed x4 -> x3, waiting for transfers between devices: 83.7 us -> 88.2 us
    unnamed x36 -> x38, local copies, waits for them, and re-layouts: 13.1 us -> 13.1 us
  transfers between devices with their start and end apart: 3 -> 5, of which waited for: 3 -> 5; matrix products, arithmetic and copies ran while one was open for 1% -> 1% of each run, Pallas kernels for 0% -> 0%
where the time goes in v1:
time: 463 us; the launch traced here: 460 us
  blocking collectives  189 us (41%)
  waiting for transfers between devices  128 us (28%)
  local copies, waits for them, and re-layouts  58.1 us (13%)
  other arithmetic  44 us (10%)
  matrix products  17.4 us (4%)
  between operations  14.4 us (3%)
  starting transfers between devices  8.15 us (2%)
    unnamed x3, waiting for transfers between devices  88.2 us
    all_gather x1, blocking collectives, shards(): lax.all_gather(expert_share[None], ('seq', 'head'), axis=0, tiled=True)  73.4 us
    pmax x1, blocking collectives, shards(): top_logit = lax.pmax(jnp.max(logits, axis=-1), 'seq')  65.3 us
    all_gather x2, blocking collectives, joined(): gathered = jax.tree.map(lambda a: lax.all_gather(a, axis), part)  50.3 us
    ppermute x3, waiting for transfers between devices, open_points(): all_rows = ppermute(part_now, row_axis, step_out(1 << p))  39.4 us
    dynamic_slice x34, local copies, waits for them, and re-layouts, take(): lax.dynamic_index_in_dim(a, source, 0, False)  28.9 us
    add x31, other arithmetic, join_three(): mass = earlier_part[1] * lead_scale + later_part[1] * trail_scale  21.8 us
    add x31, other arithmetic, join_three(): earlier_part[2] * lead_scale[..., None]  18.8 us
  transfers between devices with their start and end apart: 5, of which 5 were waited for; matrix products, arithmetic and copies ran while one was open for 1% of the time, Pallas kernels for 0%

profile of v1, /device:TPU:32, one launch (start us, length us, event | category | flops | bytes accessed | tf_op | source)
XLA Modules:
  0.0 460.0 jit_solution(9163968570619371912)
XLA Ops:
  7.3 1.2 fusion.11
  8.5 0.7 iota_add_fusion
  9.2 1.3 convolution_convert_fusion.2
  10.7 1.3 convolution_convert_fusion.1
  12.3 4.6 %copy.74 = bf16[24,512,128]{1,2,0:T(8,128)(2,1)} copy(bf16[24,512,128]{2,1,0:T(8,128)(2,1)} %param.23) | data formatting | bytes 6291456 | tf_op args[2]
  17.0 4.7 %copy.77 = bf16[24,512,128]{1,2,0:T(8,128)(2,1)} copy(bf16[24,512,128]{2,1,0:T(8,128)(2,1)} %param.24) | data formatting | bytes 6291456 | tf_op args[3]
  22.0 2.0 fusion.4
  24.0 3.1 convert_select_fusion.1
  27.1 1.0 convert_select_fusion
  28.8 3.3 convolution_bitcast_fusion.1
  32.5 25.2 %all-gather.1 = f32[768,4,2]{1,2,0:T(2,128)S(1)} all-gather(f32[24,4,2]{1,2,0:T(2,128)S(1)} %fusion.14), channel_id=3, replica_groups=mesh['seq'=32,'head'=8] {'seq'}, dimensions={0}, use_global_device_ids=true | all-gather | bytes 25344 | tf_op jit(solution)/shard_map/all_gather | solution.py:25
  58.4 25.1 %all-gather = f32[768,4,2]{1,2,0:T(2,128)S(1)} all-gather(f32[24,4,2]{1,2,0:T(2,128)S(1)} %get-tuple-element.240), channel_id=2, replica_groups=mesh['seq'=32,'head'=8] {'seq'}, dimensions={0}, use_global_device_ids=true | all-gather | bytes 25344 | tf_op jit(solution)/shard_map/all_gather | solution.py:25
  83.6 1.2 copy.83
  84.8 0.8 all-gather.6.cloned.1.call-done
  85.6 0.9 slice.42
  86.6 76.0 %while.19 = (s32[]{:T(128)}, f32[24,4,2]{0,2,1:T(2,128)S(1)}, f32[24,4,2]{0,2,1:T(2,128)S(1)}, f32[24,4,2,64]{3,2,1,0:T(2,128)S(1)}, f32[32,24,4,2]{1,3,2,0:T(2,...) while((s32[]{:T(128)}, f32[24,4,2]{0,2,1:T(2,128)S(1)}, ...), condition=%wide.region_5.6_spmd, body=%wide.region_4.5_spmd.sunk | while | flops 38021 | bytes 256655 | solution.py:30
  87.5 0.9 constant_dynamic-slice_fusion.6
  90.0 0.9 constant_dynamic-slice_fusion.6
  92.4 0.9 constant_dynamic-slice_fusion.6
  94.9 0.9 constant_dynamic-slice_fusion.6
  97.3 0.9 constant_dynamic-slice_fusion.6
  99.8 0.9 constant_dynamic-slice_fusion.6
  102.3 0.9 constant_dynamic-slice_fusion.6
  104.7 0.9 constant_dynamic-slice_fusion.6
  107.2 0.9 constant_dynamic-slice_fusion.6
  109.6 0.9 constant_dynamic-slice_fusion.6
  112.1 0.9 constant_dynamic-slice_fusion.6
  114.5 0.9 constant_dynamic-slice_fusion.6
  117.0 0.9 constant_dynamic-slice_fusion.6
  119.4 0.9 constant_dynamic-slice_fusion.6
  121.0 0.7 fusion.97
  121.9 0.9 constant_dynamic-slice_fusion.6
  124.4 0.9 constant_dynamic-slice_fusion.6
  126.8 0.9 constant_dynamic-slice_fusion.6
  129.3 0.9 constant_dynamic-slice_fusion.6
  131.7 0.9 constant_dynamic-slice_fusion.6
  134.1 0.9 constant_dynamic-slice_fusion.6
  136.6 0.9 constant_dynamic-slice_fusion.6
  139.0 0.9 constant_dynamic-slice_fusion.6
  141.5 0.9 constant_dynamic-slice_fusion.6
  143.9 0.9 constant_dynamic-slice_fusion.6
  146.4 0.9 constant_dynamic-slice_fusion.6
  148.8 0.9 constant_dynamic-slice_fusion.6
  151.3 0.9 constant_dynamic-slice_fusion.6
  153.7 0.9 constant_dynamic-slice_fusion.6
  156.2 0.9 constant_dynamic-slice_fusion.6
  158.6 0.9 constant_dynamic-slice_fusion.6
  161.1 0.9 constant_dynamic-slice_fusion.6
  164.7 10.0 %collective-permute-done = f32[96,1024]{1,0:T(8,128)S(1)} collective-permute-done((f32[96,1024]{1,0:T(8,128)S(1)}, f32[96,1024]{1,0:T(8,128)S(1)}, u32[]{:S(2)}, u32[]{:S(2)}) %collective-permute-start) | collective-permute-done | bytes 393248 | tf_op jit(solution)/shard_map/ppermute | solution.py:16
  174.8 2.2 collective-permute-start.1
  177.2 16.2 %collective-permute-done.1 = f32[96,1024]{1,0:T(8,128)S(1)} collective-permute-done((f32[96,1024]{1,0:T(8,128)S(1)}, f32[96,1024]{1,0:T(8,128)S(1)}, u32[]{:S(2)}, u32[]{:S(2)}) %collective-permute-start.1) | collective-permute-done | bytes 393248 | tf_op jit(solution)/shard_map/ppermute | solution.py:16
  193.4 5.2 %collective-permute-start.2 = (f32[96,1024]{1,0:T(8,128)S(1)}, f32[96,1024]{1,0:T(8,128)S(1)}, u32[]{:S(2)}, u32[]{:S(2)}) collective-permute-start(f32[96,1024]{1,0:T(8,128)S(1)} %add.242), channel_id=1, source_target_pairs={{0,4},{1,5},{2,6},{3,7},{4,0},{5,1},{6,2},{7,3},{8,12},{9,13},{10,... | collective-permute-start | bytes 1179656 | tf_op jit(solution)/shard_map/ppermute | solution.py:16
  198.6 13.2 %collective-permute-done.2 = f32[96,1024]{1,0:T(8,128)S(1)} collective-permute-done((f32[96,1024]{1,0:T(8,128)S(1)}, f32[96,1024]{1,0:T(8,128)S(1)}, u32[]{:S(2)}, u32[]{:S(2)}) %collective-permute-start.2) | collective-permute-done | bytes 393248 | tf_op jit(solution)/shard_map/ppermute | solution.py:16
  212.0 1.3 fusion.29
  213.8 1.0 fusion.10
  214.9 1.3 copy.98
  216.2 1.4 reshape.208
  217.8 88.2 %reduce-scatter.4.cloned.1.call-done = f32[32,32]{1,0:T(8,128)} async-done(((f32[1024,32]{1,0:T(8,128)}), f32[32,32]{1,0:T(8,128)}) %reduce-scatter.4.cloned.1.call-update) | async-done | bytes 4112
  306.0 0.8 reshape.209
  306.9 73.4 %all-gather.3 = bf16[512,16,32]{2,1,0:T(8,128)(2,1)S(1)} all-gather(bf16[2,16,32]{2,1,0:T(8,128)(2,1)S(1)} %copy.99), channel_id=5, replica_groups=mesh['seq'=32,'head'=8] {'seq','head'}, dimensions={0}, use_global_device_ids=true | all-gather | bytes 526336 | tf_op jit(solution)/shard_map/all_gather | solution.py:181
  380.3 2.7 copy.112
  383.0 3.5 reshape.189
  387.1 0.8 convolution_reduce_fusion
  387.9 65.3 %pmax.7 = f32[12]{0:T(128)} all-reduce(f32[12]{0:T(128)S(1)} %convolution_reduce_fusion), channel_id=1, replica_groups=mesh['seq'=32,'head'=8] {'seq'}, use_global_device_ids=true, to_apply=%region_14.15 | all-reduce | flops 12 | bytes 96 | tf_op jit(solution)/shard_map/pmax | solution.py:207
  (208 shorter events, 53.2 us)
Async XLA Ops:
  7.2 379.9 %copy-start = (bf16[1024,1004]{0,1:T(8,128)(2,1)S(1)}, bf16[1024,1004]{0,1:T(8,128)(2,1)}, u32[]{:S(2)}) copy-start(bf16[1024,1004]{0,1:T(8,128)(2,1)} %param.39) | copy-start | bytes 6168580
  7.2 4.8 %copy-start.2 = (bf16[96,1024]{1,0:T(8,128)(2,1)S(1)}, bf16[96,1024]{1,0:T(8,128)(2,1)}, u32[]{:S(2)}) copy-start(bf16[96,1024]{1,0:T(8,128)(2,1)} %param.21) | copy-start | bytes 589828
  7.2 4.8 %copy-start.13 = (f32[1024]{0:T(1024)S(1)}, f32[1024]{0:T(1024)}, u32[]{:S(2)}) copy-start(f32[1024]{0:T(1024)} %param.26) | copy-start | bytes 12292
  7.2 4.8 %copy-start.11 = (bf16[1024,128]{1,0:T(8,128)(2,1)S(1)}, bf16[1024,128]{1,0:T(8,128)(2,1)}, u32[]{:S(2)}) copy-start(bf16[1024,128]{1,0:T(8,128)(2,1)} %param.28) | copy-start | bytes 786436
  7.2 78.4 %all-gather.6.cloned.1.call-start = ((), (), s32[]{:S(2)}) async-start(), calls=%async_computation.1 | async-start | bytes 3244032 | tf_op jit(solution)/shard_map/all_gather | solution.py:25
  16.9 5.0 %copy-start.12 = (s32[24,4,512]{2,1,0:T(4,128)S(1)}, s32[24,4,512]{2,1,0:T(4,128)}, u32[]{:S(2)}) copy-start(s32[24,4,512]{2,1,0:T(4,128)} %param.25) | copy-start | bytes 589828
  17.0 5.0 %copy-start.15 = (f32[32,2]{0,1:T(2,128)S(1)}, f32[32,2]{0,1:T(2,128)}, u32[]{:S(2)}) copy-start(f32[32,2]{0,1:T(2,128)} %param.30) | copy-start | bytes 772
  24.0 3.1 copy-start.1
  32.1 273.9 %reduce-scatter.4.cloned.1.call-start = ((), (), s32[]{:S(2)}) async-start(), calls=%async_computation.2 | async-start | bytes 540672
  58.4 104.7 %copy-start.6 = (bf16[128,1024]{1,0:T(8,128)(2,1)S(1)}, bf16[128,1024]{1,0:T(8,128)(2,1)}, u32[]{:S(2)}) copy-start(bf16[128,1024]{1,0:T(8,128)(2,1)} %param.31) | copy-start | bytes 786436
  83.6 80.4 %copy-start.8 = (s32[4,24,2]{1,2,0:T(2,128)S(1)}, s32[4,24,2]{1,2,0:T(2,128)}, u32[]{:S(2)}) copy-start(s32[4,24,2]{1,2,0:T(2,128)} %param.37) | copy-start | bytes 2308
  162.6 49.4 %copy-start.14 = (f32[1024]{0:T(1024)S(1)}, f32[1024]{0:T(1024)}, u32[]{:S(2)}) copy-start(f32[1024]{0:T(1024)} %param.32) | copy-start | bytes 12292
  163.4 11.3 %collective-permute-start = (f32[96,1024]{1,0:T(8,128)S(1)}, f32[96,1024]{1,0:T(8,128)S(1)}, u32[]{:S(2)}, u32[]{:S(2)}) collective-permute-start(f32[96,1024]{1,0:T(8,128)S(1)} %fusion.75), channel_id=1, source_target_pairs={{0,1},{1,0},{2,3},{3,2},{4,5},{5,4},{6,7},{7,6},{8,9},{9,8},{10,11... | collective-permute-start | bytes 1179656 | tf_op jit(solution)/shard_map/ppermute | solution.py:16
  164.7 48.9 %copy-start.5 = (bf16[2,1024,88]{1,2,0:T(8,128)(2,1)S(1)}, bf16[2,1024,88]{1,2,0:T(8,128)(2,1)}, u32[]{:S(2)}) copy-start(bf16[2,1024,88]{1,2,0:T(8,128)(2,1)} %param.34) | copy-start | bytes 1081348
  174.7 39.1 %copy-start.3 = (bf16[2,88,1024]{2,1,0:T(8,128)(2,1)S(1)}, bf16[2,88,1024]{2,1,0:T(8,128)(2,1)}, u32[]{:S(2)}) copy-start(bf16[2,88,1024]{2,1,0:T(8,128)(2,1)} %param.36) | copy-start | bytes 1081348
  174.8 39.1 %copy-start.4 = (bf16[2,1024,88]{1,2,0:T(8,128)(2,1)S(1)}, bf16[2,1024,88]{1,2,0:T(8,128)(2,1)}, u32[]{:S(2)}) copy-start(bf16[2,1024,88]{1,2,0:T(8,128)(2,1)} %param.35) | copy-start | bytes 1081348
  174.8 18.6 %collective-permute-start.1 = (f32[96,1024]{1,0:T(8,128)S(1)}, f32[96,1024]{1,0:T(8,128)S(1)}, u32[]{:S(2)}, u32[]{:S(2)}) collective-permute-start(f32[96,1024]{1,0:T(8,128)S(1)} %add.241), channel_id=1, source_target_pairs={{0,2},{1,3},{2,0},{3,1},{4,6},{5,7},{6,4},{7,5},{8,10},{9,11},{10,... | collective-permute-start | bytes 1179656 | tf_op jit(solution)/shard_map/ppermute | solution.py:16
  193.4 18.4 %collective-permute-start.2 = (f32[96,1024]{1,0:T(8,128)S(1)}, f32[96,1024]{1,0:T(8,128)S(1)}, u32[]{:S(2)}, u32[]{:S(2)}) collective-permute-start(f32[96,1024]{1,0:T(8,128)S(1)} %add.242), channel_id=1, source_target_pairs={{0,4},{1,5},{2,6},{3,7},{4,0},{5,1},{6,2},{7,3},{8,12},{9,13},{10,... | collective-permute-start | bytes 1179656 | tf_op jit(solution)/shard_map/ppermute | solution.py:16
  380.3 6.8 %copy-start.9 = (f32[1024]{0:T(1024)S(1)}, f32[1024]{0:T(1024)}, u32[]{:S(2)}) copy-start(f32[1024]{0:T(1024)} %param.38) | copy-start | bytes 12292
  387.1 66.1 %copy-start.7 = (bf16[12,1024]{1,0:T(8,128)(2,1)}, bf16[12,1024]{1,0:T(8,128)(2,1)S(1)}, u32[]{:S(2)}) copy-start(bf16[12,1024]{1,0:T(8,128)(2,1)S(1)} %get-tuple-element.243) | copy-start | bytes 73732
  387.1 66.1 %copy-start.10 = (f32[12]{0:T(128)}, f32[12]{0:T(128)S(1)}, u32[]{:S(2)}) copy-start(f32[12]{0:T(128)S(1)} %add_sqrt_fusion) | copy-start | bytes 148
Sparse Core Ops, SparseCore 0:
  32.2 53.4 all-gather.5
  217.7 88.1 reduce-scatter.3
